TPU v7x, 32 devices: a whole 2x2x4 slice. The times are simulated.
32 devices in a mesh: space: 16 (over z, y, core), chan: 2 (over x).
Axes of the slice: x: 2, y: 2, z: 4, core: 2. Of those that a mesh axis runs over, the one named last changes fastest.
Arguments:
- volume: float32 [32, 32, 128, 128], P('chan', 'space'), may hold values from -6 to 6
- filters: float32 [64, 32, 3, 3, 3], P(None, 'chan'), may hold values from -0.21875 to 0.21875
- cotangent: float32 [64, 16, 64, 64], P('chan', 'space'), may hold values from -6 to 6
Outputs:
- activated: float32 [64, 16, 64, 64], P('chan', 'space')
- volume_grad: float32 [32, 32, 128, 128], P('chan', 'space')
- filter_grad: float32 [64, 32, 3, 3, 3], P(None, 'chan')
All inputs are finite; a program needn't handle non-finite values.
Results may differ from a plain program's by a relative error of at most 0.00014.
Values sent between devices are 32-bit elements; how exact they have to be, the bound alone decides.
No kernel may reach another device: no remote copies, remote signals or barrier semaphores. Data moves between devices by JAX's collectives and lax.ppermute only.
A program may use at most 192 MiB of HBM per device.

v0:
```python
import jax
import jax.numpy as jnp
from jax import lax
from jax.sharding import PartitionSpec as P


def from_behind(value, axis, steps):
    count = lax.axis_size(axis)
    initial, last = (max(0, -steps), min(count, count - steps))
    return lax.ppermute(value, axis, [(source, source + steps) for source in range(initial, last)])


def conv_local(extended, filters):
    result = lax.conv_general_dilated(
        extended[None],
        filters,
        (2, 2, 2),
        ((0, 0), (1, 1), (1, 1)),
        dimension_numbers=("NCDHW", "OIDHW", "NCDHW"),
        precision=lax.Precision.HIGHEST,
    )
    return result[0]


def on_device(volume, filters, cotangent):
    out_rows = cotangent.shape[0]
    top_plane = volume[:, -1]
    below = from_behind(top_plane, "space", 1)
    extended = jnp.concatenate([below[:, None], volume], axis=1)
    every_filter = lax.all_gather(filters, "chan", axis=1, tiled=True)
    own_filters = lax.dynamic_slice_in_dim(
        every_filter, lax.axis_index("chan") * out_rows, out_rows, 0
    )
    initial = jnp.zeros(cotangent.shape, jnp.float32)
    chosen = own_filters
    preact = initial + conv_local(lax.all_gather(extended, "chan", axis=0, tiled=True), chosen)
    activated = jax.nn.softplus(preact)
    preact_grad = cotangent * jax.nn.sigmoid(preact)
    piece = lax.all_gather(preact_grad, "chan", axis=0, tiled=True)
    start = jnp.int32(0)
    grad_filters = jnp.zeros(filters.shape, jnp.float32)
    chosen = lax.dynamic_slice_in_dim(filters, start, piece.shape[0], 0)
    unused, pullback = jax.vjp(conv_local, extended, chosen)
    grad_piece, grad_rows = pullback(piece)
    grad_extended, grad_filters = (
        grad_piece,
        lax.dynamic_update_slice_in_dim(grad_filters, grad_rows, start, 0),
    )
    spilled = from_behind(grad_extended[:, 0], "space", -1)
    volume_grad = grad_extended[:, 1:]
    volume_grad = volume_grad.at[:, -1].add(spilled)
    summed = lax.psum(grad_filters, "space")
    depth_all = volume.shape[1] * lax.axis_size("space")
    factor = float(depth_all // 2 * (volume.shape[2] // 2) * (volume.shape[3] // 2)) ** (-0.5)
    return (activated, volume_grad, summed * factor)


def solution(mesh):
    in_specs = (
        P("chan", "space", None, None),
        P(None, "chan", None, None, None),
        P("chan", "space", None, None),
    )
    out_specs = (
        P("chan", "space", None, None),
        P("chan", "space", None, None),
        P(None, "chan", None, None, None),
    )
    return jax.shard_map(
        on_device, mesh=mesh, in_specs=in_specs, out_specs=out_specs, check_vma=False
    )
```

profile of v0, /device:TPU:8, one launch (start us, length us, event | category | flops | bytes accessed | tf_op | source)
XLA Modules:
  0.0 647.2 jit_solution(8381787127257969497)
XLA Ops:
  7.2 2.4 slice_bitcast_fusion.3
  9.7 1.9 collective-permute-start
  11.6 8.6 %copy.48 = f32[16,2,128,128]{0,3,2,1:T(8,128)} copy(f32[16,2,128,128]{3,2,1,0:T(8,128)S(1)} %copy-done) | data formatting | bytes 4194304 | tf_op args[0]
  20.1 6.7 %collective-permute-done = f32[16,128,128]{2,1,0:T(8,128)S(1)} collective-permute-done((f32[16,128,128]{2,1,0:T(8,128)}, f32[16,128,128]{2,1,0:T(8,128)S(1)}, u32[]{:S(2)}, u32[]{:S(2)}) %collective-permute-start) | collective-permute-done | bytes 1048608 | tf_op jit(solution)/shard_map/ppermute | solution.py:10
  26.9 4.6 copy.47
  31.5 18.6 %pad_maximum_fusion = f32[16,3,128,128]{0,3,2,1:T(8,128)} fusion(f32[16,2,128,128]{0,3,2,1:T(8,128)} %copy.48, f32[16,1,128,128]{0,3,2,1:T(8,128)} %bitcast.46), kind=kLoop, calls=%fused_computation.6 | loop fusion | flops 786432 | bytes 6291456 | tf_op jit(solution)/shard_map/concatenate | solution.py:29
  50.1 16.0 %copy.49 = f32[16,3,128,128]{3,2,1,0:T(8,128)} copy(f32[16,3,128,128]{0,3,2,1:T(8,128)} %pad_maximum_fusion) | data formatting | bytes 6291456 | tf_op jit(solution)/shard_map/concatenate | solution.py:29
  68.2 7.1 %all_gather.10 = f32[64,32,3,3,3]{0,1,4,3,2:T(8,128)S(1)} all-gather(f32[64,16,3,3,3]{0,1,4,3,2:T(8,128)S(1)} %copy-done.2), channel_id=1, replica_groups=mesh['space'=16,'chan'=2] {'chan'}, dimensions={1}, use_global_device_ids=true | all-gather | bytes 331776 | tf_op jit(solution)/shard_map/all_gather | solution.py:30
  75.3 71.6 %all-gather.3.cloned.1.call-done = f32[32,3,128,128]{3,2,1,0:T(8,128)} async-done(((f32[16,3,128,128]{3,2,1,0:T(8,128)}), f32[32,3,128,128]{3,2,1,0:T(8,128)}) %all-gather.3.cloned.1.call-update) | async-done | bytes 6291472 | tf_op jit(solution)/shard_map/all_gather | solution.py:36
  146.9 6.7 %copy.50 = f32[32,3,128,128]{2,0,3,1:T(8,128)} copy(f32[32,3,128,128]{3,2,1,0:T(8,128)} %all-gather.3.cloned.1.call-done) | data formatting | bytes 12582912 | tf_op jit(solution)/shard_map/all_gather | solution.py:36
  153.6 6.7 %pad.2 = f32[32,3,128,1,144]{2,0,4,1,3:T(8,128)} pad(f32[32,3,128,1,128]{2,0,4,1,3:T(8,128)} %bitcast.48, f32[]{:T(128)} %constant.42.clone.1), padding=0_0x0_0x0_0x0_0x1_15 | pad | bytes 13369348 | tf_op jit(solution)/shard_map/broadcast_in_dim | solution.py:15
  160.3 24.8 %copy.52 = f32[32,3,128,1,8,18]{0,4,5,2,1,3:T(8,128)} copy(f32[32,3,128,1,8,18]{2,0,5,4,1,3:T(8,128)} %bitcast.47) | data formatting | bytes 14155776 | tf_op jit(solution)/shard_map/conv_general_dilated | solution.py:14
  185.1 2.2 slice.45
  187.3 37.1 %fusion.11 = f32[1,64,8,9,32]{4,2,3,1,0:T(8,128)} fusion(f32[32,3,128,1,7,2]{0,4,5,2,1,3:T(8,128)S(1)} %slice.45, f32[32,3,128,1,8,18]{0,4,5,2,1,3:T(8,128)} %copy.52, pred[8,9]{0,1:T(8,128)(4,1)S(1)} %copy-done.4, f32[64,32,3,3,3]{0,1,4,3,2:T(8,128)S(1)} %all_gather.10, s32[]{:T(128)S(6)} %select_n.15), kind=kOutput, calls=%fused_computation.17 | convolution fusion | flops 1526906880 | bytes 8577100 | tf_op jit(solution)/shard_map/conv_general_dilated | solution.py:14
  224.4 2.2 copy.54
  226.7 1.7 divide_multiply_fusion
  228.4 1.6 copy.56
  230.0 33.2 %all-gather.5.cloned.1.call-done = f32[64,1,64,64]{3,2,1,0:T(8,128)} async-done(((f32[32,1,64,64]{3,2,1,0:T(8,128)}), f32[64,1,64,64]{3,2,1,0:T(8,128)}) %all-gather.5.cloned.1.call-update) | async-done | bytes 1048592 | tf_op jit(solution)/shard_map/all_gather | solution.py:39
  263.3 3.1 copy.57
  266.4 1.7 pad.4
  268.0 2.3 copy.59
  271.0 86.4 %broadcast_select_fusion = f32[3,128,8,18,16]{4,2,3,1,0:T(8,128)} fusion(pred[8,18]{0,1:T(8,128)(4,1)S(1)} %copy-done.3, f32[64,16,3,3,3]{0,1,4,3,2:T(8,128)S(1)} %copy-done.2, f32[64,1,64,8,10]{0,3,4,2,1:T(8,128)S(1)} %fusion.32), kind=kOutput, calls=%fused_computation.9 | convolution fusion | flops 1521745920 | bytes 4960400 | tf_op jit(solution)/shard_map/transpose(jvp())/conv_general_dilated | solution.py:14
  357.4 17.2 %copy.60 = f32[3,128,8,18,16]{1,4,3,2,0:T(8,128)} copy(f32[3,128,8,18,16]{4,2,3,1,0:T(8,128)} %broadcast_select_fusion) | data formatting | bytes 7077888 | tf_op jit(solution)/shard_map/transpose(jvp())/conv_general_dilated | solution.py:14
  374.7 2.1 slice_bitcast_fusion
  377.8 2.8 collective-permute-start.1
  380.6 3.3 copy.61
  383.9 159.1 %fusion.25 = f32[64,16,3,3,3]{0,1,4,3,2:T(8,128)} fusion(f32[1,16,3,128,128]{1,0,4,3,2:T(1,128)} %bitcast.45, f32[1,64,1,64,64]{1,0,4,3,2:T(1,128)} %bitcast.53), kind=kOutput, calls=%fused_computation.35 | convolution fusion | flops 1344835584 | bytes 4304896 | tf_op jit(solution)/shard_map/transpose(jvp())/conv_general_dilated | solution.py:14
  543.1 2.7 copy.62
  547.3 86.3 %all-reduce.2.cloned.1.call-done = f32[64,16,3,3,3]{0,1,4,3,2:T(8,128)} async-done(((f32[64,16,3,3,3]{0,1,4,3,2:T(8,128)}), f32[64,16,3,3,3]{0,1,4,3,2:T(8,128)}) %all-reduce.2.cloned.1.call-update) | async-done | bytes 110608 | tf_op jit(solution)/shard_map/psum | solution.py:52
  633.6 1.6 broadcast_multiply_fusion
  635.2 2.4 fusion.16
  637.6 2.9 copy.63
  (22 shorter events, 5.4 us)
Async XLA Ops:
  7.2 4.4 copy-start
  7.2 139.7 %all-gather.3.cloned.1.call-start = ((), (), s32[]{:S(2)}) async-start(), calls=%async_computation | async-start | bytes 9437184 | tf_op jit(solution)/shard_map/all_gather | solution.py:36
  9.7 17.2 %collective-permute-start = (f32[16,128,128]{2,1,0:T(8,128)}, f32[16,128,128]{2,1,0:T(8,128)S(1)}, u32[]{:S(2)}, u32[]{:S(2)}) collective-permute-start(f32[16,128,128]{2,1,0:T(8,128)} %slice_bitcast_fusion.3), channel_id=1, source_target_pairs={{0,2},{2,4},{4,6},{6,8},{8,10},{10,12},{12,14},{14,16},{16,18},{18... | collective-permute-start | bytes 3145736 | tf_op jit(solution)/shard_map/ppermute | solution.py:10
  66.1 1.2 copy-start.1
  66.1 2.2 copy-start.2
  66.1 197.2 %all-gather.5.cloned.1.call-start = ((), (), s32[]{:S(2)}) async-start(), calls=%async_computation.1 | async-start | bytes 3145728 | tf_op jit(solution)/shard_map/all_gather | solution.py:39
  185.1 2.2 copy-start.4
  230.0 403.6 %all-reduce.2.cloned.1.call-start = ((), (), s32[]{:S(2)}) async-start(), calls=%async_computation.2 | async-start | bytes 442368 | tf_op jit(solution)/shard_map/psum | solution.py:52
  270.3 0.7 copy-start.3
  377.8 257.4 %collective-permute-start.1 = (f32[16,128,128]{1,0,2:T(8,128)}, f32[16,128,128]{1,0,2:T(8,128)}, u32[]{:S(2)}, u32[]{:S(2)}) collective-permute-start(f32[16,128,128]{1,0,2:T(8,128)} %slice_bitcast_fusion.1), channel_id=1, source_target_pairs={{2,0},{4,2},{6,4},{8,6},{10,8},{12,10},{14,12},{16,14},{18,16},{20... | collective-permute-start | bytes 3145736 | tf_op jit(solution)/shard_map/ppermute | solution.py:10
Sparse Core Ops, SparseCore 0:
  66.2 80.6 all-gather.2
  230.1 33.1 all-gather.4
  543.2 90.3 all-reduce.1
where the time goes:
time: 651 us; the launch traced here: 647 us
  matrix products  283 us (43%)
  waiting for transfers between devices  198 us (30%)
  local copies, waits for them, and re-layouts  116 us (18%)
  other arithmetic  24.5 us (4%)
  between operations  14.1 us (2%)
  blocking collectives  7.07 us (1%)
    conv_general_dilated x3, matrix products, conv_local(): lax.conv_general_dilated(extended[None], filters, (2, 2, 2), ((0, 0), (1,...  283 us
    psum x1, waiting for transfers between devices, on_device(): summed = lax.psum(grad_filters, 'space')  86.3 us
    all_gather x1, waiting for transfers between devices, on_device(): lax.all_gather(extended, 'chan', axis=0, tiled=True)  71.6 us
    conv_general_dilated x6, local copies, waits for them, and re-layouts, conv_local(): lax.conv_general_dilated(extended[None], filters, (2, 2, 2), ((0, 0), (1,...  48.8 us
    all_gather x1, waiting for transfers between devices, on_device(): piece = lax.all_gather(preact_grad, 'chan', axis=0, tiled=True)  33.2 us
    concatenate x1, other arithmetic, on_device(): extended = jnp.concatenate([below[:, None], volume], axis=1)  18.6 us
    unnamed x14, local copies, waits for them, and re-layouts  16.7 us
    concatenate x1, local copies, waits for them, and re-layouts, on_device(): extended = jnp.concatenate([below[:, None], volume], axis=1)  16 us
  transfers between devices with their start and end apart: 5, of which 4 were waited for; matrix products, arithmetic and copies ran while one was open for 27% of the time, Pallas kernels for 0%

commit v1 on v0

--- a/solution.py
+++ b/solution.py
@@ -2,6 +2,18 @@
 import jax.numpy as jnp
 from jax import lax
 from jax.sharding import PartitionSpec as P
+
+
+def collect(shard, axis, dim):
+    ways, here = (lax.axis_size(axis), lax.axis_index(axis))
+    grown, reach = (shard, 1)
+    while reach < ways:
+        theirs = lax.ppermute(grown, axis, [(d, d ^ reach) for d in range(ways)])
+        mine_first = jnp.concatenate([grown, theirs], axis=dim)
+        theirs_first = jnp.concatenate([theirs, grown], axis=dim)
+        grown = jnp.where(here & reach == 0, mine_first, theirs_first)
+        reach = 2 * reach
+    return grown
 
 
 def from_behind(value, axis, steps):
@@ -33,7 +45,7 @@
     )
     initial = jnp.zeros(cotangent.shape, jnp.float32)
     chosen = own_filters
-    preact = initial + conv_local(lax.all_gather(extended, "chan", axis=0, tiled=True), chosen)
+    preact = initial + conv_local(collect(extended, "chan", 0), chosen)
     activated = jax.nn.softplus(preact)
     preact_grad = cotangent * jax.nn.sigmoid(preact)
     piece = lax.all_gather(preact_grad, "chan", axis=0, tiled=True)

time: 651 us -> 788 us (1.21)
  other arithmetic: 24.5 us -> 136 us
  waiting for transfers between devices: 198 us -> 126 us
  blocking collectives: 7.07 us -> 70.9 us
  local copies, waits for them, and re-layouts: 116 us -> 143 us
    select_n x0 -> x1, other arithmetic: none -> 112 us  [collect(): grown = jnp.where(here & reach == 0, mine_first, theirs_first)]
    all_gather x1 -> x0, waiting for transfers between devices: 71.6 us -> none  [on_device(): lax.all_gather(extended, 'chan', axis=0, tiled=True)]
    all_gather x1, blocking collectives: 7.07 us -> 70.9 us  [on_device(): every_filter = lax.all_gather(filters, 'chan', axis=1, tiled=True)]
    unnamed x14 -> x15, local copies, waits for them, and re-layouts: 16.7 us -> 35.3 us
    ppermute x0 -> x1, local copies, waits for them, and re-layouts: none -> 14.2 us  [collect(): theirs = lax.ppermute(grown, axis, [(d, d ^ reach) for d in range(ways)])]
  transfers between devices with their start and end apart: 5 -> 5, of which waited for: 4 -> 3; matrix products, arithmetic and copies ran while one was open for 27% -> 23% of each run, Pallas kernels for 0% -> 0%
where the time goes in v1:
time: 788 us; the launch traced here: 780 us
  matrix products  283 us (36%)
  local copies, waits for them, and re-layouts  143 us (18%)
  other arithmetic  136 us (17%)
  waiting for transfers between devices  126 us (16%)
  blocking collectives  70.9 us (9%)
  between operations  14.5 us (2%)
    conv_general_dilated x3, matrix products, conv_local(): lax.conv_general_dilated(extended[None], filters, (2, 2, 2), ((0, 0), (1,...  283 us
    select_n x1, other arithmetic, collect(): grown = jnp.where(here & reach == 0, mine_first, theirs_first)  112 us
    psum x1, waiting for transfers between devices, on_device(): summed = lax.psum(grad_filters, 'space')  86.3 us
    all_gather x1, blocking collectives, on_device(): every_filter = lax.all_gather(filters, 'chan', axis=1, tiled=True)  70.9 us
    conv_general_dilated x6, local copies, waits for them, and re-layouts, conv_local(): lax.conv_general_dilated(extended[None], filters, (2, 2, 2), ((0, 0), (1,...  48.8 us
    unnamed x15, local copies, waits for them, and re-layouts  35.3 us
    all_gather x1, waiting for transfers between devices, on_device(): piece = lax.all_gather(preact_grad, 'chan', axis=0, tiled=True)  33.4 us
    concatenate x1, other arithmetic, on_device(): extended = jnp.concatenate([below[:, None], volume], axis=1)  18.6 us
  transfers between devices with their start and end apart: 5, of which 3 were waited for; matrix products, arithmetic and copies ran while one was open for 23% of the time, Pallas kernels for 0%

profile of v1, /device:TPU:8, one launch (start us, length us, event | category | flops | bytes accessed | tf_op | source)
XLA Modules:
  0.0 779.8 jit_solution(6693386760902949660)
XLA Ops:
  7.2 2.4 slice_bitcast_fusion.3
  9.7 1.9 collective-permute-start
  11.6 8.7 %copy.51 = f32[16,2,128,128]{0,3,2,1:T(8,128)} copy(f32[16,2,128,128]{3,2,1,0:T(8,128)S(1)} %copy-done) | data formatting | bytes 4194304 | tf_op args[0]
  20.2 6.6 collective-permute-done
  26.9 4.6 copy.50
  31.5 18.6 %pad_maximum_fusion = f32[16,3,128,128]{0,3,2,1:T(8,128)} fusion(f32[16,2,128,128]{0,3,2,1:T(8,128)} %copy.51, f32[16,1,128,128]{0,3,2,1:T(8,128)} %bitcast.50), kind=kLoop, calls=%fused_computation.7 | loop fusion | flops 786432 | bytes 6291456 | tf_op jit(solution)/shard_map/concatenate | solution.py:41
  50.1 16.1 %copy.52 = f32[16,3,128,128]{3,2,1,0:T(8,128)} copy(f32[16,3,128,128]{0,3,2,1:T(8,128)} %pad_maximum_fusion) | data formatting | bytes 6291456 | tf_op jit(solution)/shard_map/concatenate | solution.py:41
  68.6 70.9 %all_gather.6 = f32[64,32,3,3,3]{0,1,4,3,2:T(8,128)S(1)} all-gather(f32[64,16,3,3,3]{0,1,4,3,2:T(8,128)S(1)} %copy-done.2), channel_id=1, replica_groups=mesh['space'=16,'chan'=2] {'chan'}, dimensions={1}, use_global_device_ids=true | all-gather | bytes 331776 | tf_op jit(solution)/shard_map/all_gather | solution.py:42
  139.5 14.2 %copy.53 = f32[16,3,128,128]{0,3,2,1:T(8,128)} copy(f32[16,3,128,128]{3,2,1,0:T(8,128)} %collective-permute-done.1) | data formatting | bytes 6291456 | tf_op jit(solution)/shard_map/ppermute | solution.py:11
  153.7 111.5 %broadcast_select_fusion = f32[1,32,3,128,128]{1,0,4,3,2:T(1,128)} fusion(pred[]{:T(512)S(6)} %eq.3, f32[1,16,3,128,128]{1,0,4,3,2:T(1,128)} %bitcast.48, f32[1,16,3,128,128]{1,0,4,3,2:T(1,128)} %bitcast.46), kind=kLoop, calls=%fused_computation | loop fusion | flops 4718592 | bytes 12582913 | tf_op jit(solution)/shard_map/jit(_where)/select_n | solution.py:14
  265.2 19.6 %copy.70 = f32[32,3,128,1,128]{2,0,4,1,3:T(8,128)} copy(f32[32,3,128,1,128]{0,4,2,1,3:T(8,128)} %bitcast.49) | data formatting | bytes 12582912
  284.8 6.7 pad.2.clone
  291.6 24.8 %copy.56 = f32[32,3,128,1,8,18]{0,4,5,2,1,3:T(8,128)} copy(f32[32,3,128,1,8,18]{2,0,5,4,1,3:T(8,128)} %bitcast.51) | data formatting | bytes 14155776 | tf_op jit(solution)/shard_map/conv_general_dilated | solution.py:26
  316.4 2.2 slice.45
  318.6 37.6 %fusion.11 = f32[1,64,8,9,32]{4,2,3,1,0:T(8,128)} fusion(f32[32,3,128,1,7,2]{0,4,5,2,1,3:T(8,128)S(1)} %slice.45, f32[32,3,128,1,8,18]{0,4,5,2,1,3:T(8,128)} %copy.56, pred[8,9]{0,1:T(8,128)(4,1)S(1)} %copy-done.4, f32[64,32,3,3,3]{0,1,4,3,2:T(8,128)S(1)} %all_gather.6, s32[]{:T(128)S(6)} %select_n.32), kind=kOutput, calls=%fused_computation.18 | convolution fusion | flops 1526906880 | bytes 8577100 | tf_op jit(solution)/shard_map/conv_general_dilated | solution.py:26
  356.1 2.2 copy.58
  358.4 1.8 divide_multiply_fusion
  361.8 33.4 %all-gather.2.cloned.1.call-done = f32[64,1,64,64]{3,2,1,0:T(8,128)} async-done(((f32[32,1,64,64]{3,2,1,0:T(8,128)}), f32[64,1,64,64]{3,2,1,0:T(8,128)}) %all-gather.2.cloned.1.call-update) | async-done | bytes 1048592 | tf_op jit(solution)/shard_map/all_gather | solution.py:51
  395.3 3.1 copy.61
  398.4 1.8 pad.4
  400.1 2.3 copy.63
  403.1 86.3 %broadcast_select_fusion.1 = f32[3,128,8,18,16]{4,2,3,1,0:T(8,128)} fusion(pred[8,18]{0,1:T(8,128)(4,1)S(1)} %copy-done.3, f32[64,16,3,3,3]{0,1,4,3,2:T(8,128)S(1)} %copy-done.2, f32[64,1,64,8,10]{0,3,4,2,1:T(8,128)S(1)} %fusion.32), kind=kOutput, calls=%fused_computation.10 | convolution fusion | flops 1521745920 | bytes 4960400 | tf_op jit(solution)/shard_map/transpose(jvp())/conv_general_dilated | solution.py:26
  489.5 17.2 %copy.64 = f32[3,128,8,18,16]{1,4,3,2,0:T(8,128)} copy(f32[3,128,8,18,16]{4,2,3,1,0:T(8,128)} %broadcast_select_fusion.1) | data formatting | bytes 7077888 | tf_op jit(solution)/shard_map/transpose(jvp())/conv_general_dilated | solution.py:26
  506.7 2.1 slice_bitcast_fusion
  510.0 2.8 collective-permute-start.2
  512.8 3.3 copy.65
  516.1 159.1 %fusion.25 = f32[64,16,3,3,3]{0,1,4,3,2:T(8,128)} fusion(f32[1,16,3,128,128]{1,0,4,3,2:T(1,128)} %bitcast.47, f32[1,64,1,64,64]{1,0,4,3,2:T(1,128)} %bitcast.56), kind=kOutput, calls=%fused_computation.36 | convolution fusion | flops 1344835584 | bytes 4304896 | tf_op jit(solution)/shard_map/transpose(jvp())/conv_general_dilated | solution.py:26
  675.2 2.7 copy.66
  679.4 86.3 %all-reduce.2.cloned.1.call-done = f32[64,16,3,3,3]{0,1,4,3,2:T(8,128)} async-done(((f32[64,16,3,3,3]{0,1,4,3,2:T(8,128)}), f32[64,16,3,3,3]{0,1,4,3,2:T(8,128)}) %all-reduce.2.cloned.1.call-update) | async-done | bytes 110608 | tf_op jit(solution)/shard_map/psum | solution.py:64
  765.7 1.6 broadcast_multiply_fusion
  767.4 2.4 fusion.16
  769.7 2.9 copy.67
  (23 shorter events, 7.4 us)
Async XLA Ops:
  7.2 4.4 copy-start
  7.2 388.1 %all-gather.2.cloned.1.call-start = ((), (), s32[]{:S(2)}) async-start(), calls=%async_computation | async-start | bytes 3145728 | tf_op jit(solution)/shard_map/all_gather | solution.py:51
  9.7 17.2 %collective-permute-start = (f32[16,128,128]{2,1,0:T(8,128)}, f32[16,128,128]{2,1,0:T(8,128)S(1)}, u32[]{:S(2)}, u32[]{:S(2)}) collective-permute-start(f32[16,128,128]{2,1,0:T(8,128)} %slice_bitcast_fusion.3), channel_id=1, source_target_pairs={{0,2},{2,4},{4,6},{6,8},{8,10},{10,12},{12,14},{14,16},{16,18},{18... | collective-permute-start | bytes 3145736 | tf_op jit(solution)/shard_map/ppermute | solution.py:22
  50.1 17.6 %copy-start.1 = (f32[32,1,64,64]{3,2,1,0:T(8,128)S(1)}, f32[32,1,64,64]{3,2,1,0:T(8,128)}, u32[]{:S(2)}) copy-start(f32[32,1,64,64]{3,2,1,0:T(8,128)} %param.7) | copy-start | bytes 1572868
  50.1 18.5 %copy-start.2 = (f32[64,16,3,3,3]{0,1,4,3,2:T(8,128)S(1)}, f32[64,16,3,3,3]{0,1,4,3,2:T(8,128)}, u32[]{:S(2)}) copy-start(f32[64,16,3,3,3]{0,1,4,3,2:T(8,128)} %param.6) | copy-start | bytes 331780
  66.1 73.3 %collective-permute-start.1 = (f32[16,3,128,128]{3,2,1,0:T(8,128)}, f32[16,3,128,128]{3,2,1,0:T(8,128)}, u32[]{:S(2)}, u32[]{:S(2)}) collective-permute-start(f32[16,3,128,128]{3,2,1,0:T(8,128)} %copy.52), channel_id=1, source_target_pairs={{0,1},{1,0},{2,3},{3,2},{4,5},{5,4},{6,7},{7,6},{8,9},{9,8},{10,11... | collective-permute-start | bytes 9437192 | tf_op jit(solution)/shard_map/ppermute | solution.py:11
  316.3 2.2 copy-start.4
  361.8 403.9 %all-reduce.2.cloned.1.call-start = ((), (), s32[]{:S(2)}) async-start(), calls=%async_computation.1 | async-start | bytes 442368 | tf_op jit(solution)/shard_map/psum | solution.py:64
  402.5 0.7 copy-start.3
  510.0 257.4 %collective-permute-start.2 = (f32[16,128,128]{1,0,2:T(8,128)}, f32[16,128,128]{1,0,2:T(8,128)}, u32[]{:S(2)}, u32[]{:S(2)}) collective-permute-start(f32[16,128,128]{1,0,2:T(8,128)} %slice_bitcast_fusion.1), channel_id=1, source_target_pairs={{2,0},{4,2},{6,4},{8,6},{10,8},{12,10},{14,12},{16,14},{18,16},{20... | collective-permute-start | bytes 3145736 | tf_op jit(solution)/shard_map/ppermute | solution.py:22
Sparse Core Ops, SparseCore 0:
  361.9 33.3 all-gather.1
  675.3 90.3 all-reduce.1
